TPU v7x, 512 devices: a whole 4x4x16 slice. The times are simulated.
512 devices in a mesh: segment: 4 (over x_hi, core), seq: 32 (over x_lo, z), dp: 4 (over y).
Axes of the slice: x: 4 (x_hi: 2, x_lo: 2; x = x_hi * 2 + x_lo), y: 4, z: 16, core: 2. Of those that a mesh axis runs over, the one named last changes fastest.
Arguments:
- q_in: bfloat16 [4, 4096, 1536], P('dp', 'seq', 'segment'), may hold values from -128 to 128
- k_in: bfloat16 [4, 4096, 1536], P('dp', 'seq', 'segment'), may hold values from -128 to 128
- v_in: bfloat16 [4, 4096, 1536], P('dp', 'seq', 'segment'), may hold values from -6 to 6
- q_gain: float32 [2, 64], replicated, may hold values from 1.5 to 4
- gate: float32 [768], replicated, may hold values from -6 to 6
- cot: bfloat16 [4, 4096, 768], P('dp', 'seq'), may hold values from -6 to 6
Outputs:
- attn_out: bfloat16 [4, 4096, 1536], P('dp', 'seq', 'segment')
- grad_gate: float32 [768], replicated
All inputs are finite; a program needn't handle non-finite values.
Results may differ from a plain program's by a relative error of at most 0.028.
The roundings to bfloat16 on the way count: a program that leaves them out, or rounds other values in their place, can miss the bound.
Values may be sent and summed in bfloat16 or wider, within the bound.
A program may use at most 64 MiB of HBM per device.

v0:
```python
import jax
import jax.numpy as jnp
from jax import lax
from jax.sharding import PartitionSpec as P

HEAD_DIM = 64


def shifted(value, axis, steps):
    count = lax.axis_size(axis)
    first, last = (max(0, -steps), min(count, count - steps))
    return lax.ppermute(value, axis, [(source, source + steps) for source in range(first, last)])


def attend(query, all_keys, all_values):
    count_rows = query.shape[0]
    total_keys = all_keys.shape[0]
    span = 2 * HEAD_DIM
    pieces = []
    probs_list = []
    totals_list = []
    for offset in range(0, query.shape[1], span):
        query_group = query[:, offset : offset + span].reshape(count_rows, 2, HEAD_DIM)
        keys_group = all_keys[:, offset : offset + span].reshape(total_keys, 2, HEAD_DIM)
        values_group = all_values[:, offset : offset + span].reshape(total_keys, 2, HEAD_DIM)
        scores = jnp.einsum(
            "qhd,khd->hqk", query_group, keys_group, preferred_element_type=jnp.float32
        ) * HEAD_DIM ** (-0.5)
        peak = jnp.max(scores, axis=-1, keepdims=True)
        expd = jnp.exp(scores - peak)
        total = jnp.sum(expd, axis=-1, keepdims=True)
        probs = expd.astype(jnp.bfloat16)
        result = jnp.einsum("hqk,khd->qhd", probs, values_group, preferred_element_type=jnp.float32)
        result = result / jnp.transpose(total, (1, 0, 2))
        pieces.append(result.reshape(count_rows, span))
        probs_list.append(probs)
        totals_list.append(total)
    return (jnp.concatenate(pieces, axis=1), probs_list, totals_list)


def attend_back(probs_list, totals_list, normed, upstream, all_keys, all_values):
    count_rows = upstream.shape[0]
    total_keys = all_keys.shape[0]
    span = 2 * HEAD_DIM
    pieces = []
    for number in range(len(probs_list)):
        offset = number * span
        upstream_group = upstream[:, offset : offset + span].reshape(count_rows, 2, HEAD_DIM)
        normed_group = normed[:, offset : offset + span].reshape(count_rows, 2, HEAD_DIM)
        keys_group = all_keys[:, offset : offset + span].reshape(total_keys, 2, HEAD_DIM)
        values_group = all_values[:, offset : offset + span].reshape(total_keys, 2, HEAD_DIM)
        dprob = jnp.einsum(
            "qhd,khd->hqk", upstream_group, values_group, preferred_element_type=jnp.float32
        )
        delta = jnp.sum(upstream_group.astype(jnp.float32) * normed_group, axis=-1)
        delta = jnp.transpose(delta, (1, 0))[:, :, None]
        dscore = (
            probs_list[number].astype(jnp.float32) / totals_list[number] * (dprob - delta)
        ).astype(jnp.bfloat16)
        result = jnp.einsum(
            "hqk,khd->qhd", dscore, keys_group, preferred_element_type=jnp.float32
        ) * HEAD_DIM ** (-0.5)
        pieces.append(result.reshape(count_rows, span))
    return jnp.concatenate(pieces, axis=1)


def local(q_in, k_in, v_in, q_gain, gate, cot):
    half = lax.axis_size("segment") // 2
    place = lax.axis_index("segment")
    is_main = place >= half
    section = place // half
    slot = place % half
    queries = q_in[0]
    keys = k_in[0]
    values = v_in[0]
    count_rows = queries.shape[0]
    width_dev = queries.shape[1]
    all_keys, all_values = (
        lax.all_gather(keys, "seq", axis=0, tiled=True),
        lax.all_gather(values, "seq", axis=0, tiled=True),
    )
    gain_row = lax.dynamic_slice_in_dim(q_gain, section, 1, 0)[0]
    gate_part = lax.dynamic_slice_in_dim(gate, slot * width_dev, width_dev, 0)
    cot_part = lax.dynamic_slice_in_dim(cot[0], slot * width_dev, width_dev, 1)
    raw = queries.astype(jnp.float32).reshape(count_rows, width_dev // HEAD_DIM, HEAD_DIM)
    unit = raw * lax.rsqrt(jnp.mean(raw * raw, axis=-1, keepdims=True) + 1e-06)
    base = (unit * gain_row).reshape(count_rows, width_dev)

    def control_run(base_in):
        normed_c = attend(base_in.astype(jnp.bfloat16), all_keys, all_values)[0]
        return lax.optimization_barrier(normed_c.astype(jnp.bfloat16))

    def control_skip(base_in):
        return jnp.zeros((count_rows, width_dev), jnp.bfloat16)

    first = lax.cond(is_main, control_skip, control_run, base)
    first_wide = first.astype(jnp.float32)
    outgoing = (gate_part * first_wide).astype(jnp.bfloat16)
    incoming = shifted(outgoing, "segment", half)

    def main_run(incoming_in):
        query = (base + incoming_in.astype(jnp.float32)).astype(jnp.bfloat16)
        normed_m, probs_list, totals_list = attend(query, all_keys, all_values)
        dquery = attend_back(probs_list, totals_list, normed_m, cot_part, all_keys, all_values)
        return (normed_m.astype(jnp.bfloat16), dquery)

    def main_skip(incoming_in):
        return (
            jnp.zeros((count_rows, width_dev), jnp.bfloat16),
            jnp.zeros((count_rows, width_dev), jnp.float32),
        )

    final, dquery_main = lax.cond(is_main, main_run, main_skip, incoming)
    returned = shifted(dquery_main.astype(jnp.bfloat16), "segment", -half)
    returned_wide = returned.astype(jnp.float32)
    part_gate = jnp.sum(first_wide * returned_wide, axis=0)
    placed = lax.dynamic_update_slice_in_dim(
        jnp.zeros((width_dev * half,), jnp.float32), part_gate, slot * width_dev, 0
    )
    total_gate = lax.psum(placed, ("segment", "seq", "dp"))
    output = jnp.where(is_main, final, first)
    return (output[None], total_gate)


def solution(mesh):
    in_specs = (
        P("dp", "seq", "segment"),
        P("dp", "seq", "segment"),
        P("dp", "seq", "segment"),
        P(),
        P(),
        P("dp", "seq", None),
    )
    out_specs = (P("dp", "seq", "segment"), P())
    return jax.shard_map(local, mesh=mesh, in_specs=in_specs, out_specs=out_specs, check_vma=False)
```

profile of v0, /device:TPU:1, one launch (start us, length us, event | category | flops | bytes accessed | tf_op | source)
XLA Modules:
  0.0 449.7 jit_solution(1224437534765963869)
XLA Ops:
  7.2 0.0 copy-start
  7.2 0.0 all-gather.5.cloned.1.call-start
  7.2 1.6 copy.10
  8.9 0.0 all-gather.5.cloned.1.call-update
  8.9 0.0 all-gather.7.cloned.1.call-start
  8.9 1.6 copy.11
  10.6 0.0 all-gather.7.cloned.1.call-update
  10.6 0.0 copy-done
  10.6 0.1 mul.127
  10.7 1.0 copy.9
  11.8 0.1 fusion.70
  11.9 0.8 dynamic_slice.11
  12.7 116.3 %all-gather.5.cloned.1.call-done = bf16[1,4096,384]{1,2,0:T(8,128)(2,1)} async-done(((bf16[1,128,384]{1,2,0:T(8,128)(2,1)}), bf16[1,4096,384]{1,2,0:T(8,128)(2,1)}) %all-gather.5.cloned.1.call-update) | async-done | bytes 3145744 | tf_op jit(solution)/shard_map/all_gather | solution.py:79
  129.0 133.1 %all-gather.7.cloned.1.call-done = bf16[1,4096,384]{1,2,0:T(8,128)(2,1)} async-done(((bf16[1,128,384]{1,2,0:T(8,128)(2,1)}), bf16[1,4096,384]{1,2,0:T(8,128)(2,1)}) %all-gather.7.cloned.1.call-update) | async-done | bytes 3145744 | tf_op jit(solution)/shard_map/all_gather | solution.py:80
  262.1 10.9 %conditional.2 = (f32[128,384]{0,1:T(8,128)S(1)}, bf16[128,384]{1,0:T(8,128)(2,1)S(1)}) conditional(s32[]{:T(128)} %convert_element_type.105, (f32[128,384]{0,1:T(8,128)S(1)}, bf16[4096,384]{0,1:T(8,128)(2,1)}, bf16[4096,384]{0,1:T(8,128)(2,1)}) %tuple.81, () %tuple.30), branch_computations={%region_1.8_spmd, %region_8.9_spmd} | conditional | flops 824670720 | bytes 58014736 | solution.py:96
  262.1 3.2 fusion.71
  265.4 0.8 fusion.76
  266.2 0.7 fusion
  267.0 0.9 fusion.39
  267.9 0.8 fusion.75
  268.7 0.7 fusion.2
  269.4 0.9 fusion.36
  270.4 0.8 fusion.74
  271.2 0.7 fusion.4
  271.9 0.9 fusion.33
  272.9 0.1 copy.15
  273.1 0.0 copy-start.6
  273.1 0.1 multiply_convert_fusion
  273.2 1.3 collective-permute-start
  274.5 1.6 collective-permute-done
  276.1 0.0 copy-done.6
  276.1 0.9 conditional.3
  276.1 0.7 broadcast.53.clone
  277.0 1.3 collective-permute-start.1
  278.3 1.6 select_bitcast_fusion
  279.8 38.2 %collective-permute-done.1 = bf16[128,384]{0,1:T(8,128)(2,1)S(1)} collective-permute-done((bf16[128,384]{0,1:T(8,128)(2,1)S(1)}, bf16[128,384]{0,1:T(8,128)(2,1)S(1)}, u32[]{:S(2)}, u32[]{:S(2)}) %collective-permute-start.1) | collective-permute-done | bytes 98336 | tf_op jit(solution)/shard_map/ppermute | solution.py:12
  318.0 0.1 multiply_reduce_fusion.3
  318.2 0.2 dynamic_update_slice.3
  318.5 124.4 %psum.7 = f32[768]{0:T(1024)} all-reduce(f32[768]{0:T(1024)S(1)} %dynamic_update_slice.3), channel_id=1, replica_groups=mesh['segment'=4,'seq'=32,'dp'=4] {'segment','seq','dp'}, use_global_device_ids=true, to_apply=%region_21.22 | all-reduce | flops 768 | bytes 6144 | tf_op jit(solution)/shard_map/psum | solution.py:120
  (11 shorter events, 0.1 us)
Async XLA Ops:
  7.2 3.4 copy-start
  7.2 121.8 %all-gather.5.cloned.1.call-start = ((), (), s32[]{:S(2)}) async-start(), calls=%async_computation | async-start | bytes 3244032 | tf_op jit(solution)/shard_map/all_gather | solution.py:79
  8.9 253.3 %all-gather.7.cloned.1.call-start = ((), (), s32[]{:S(2)}) async-start(), calls=%async_computation.1 | async-start | bytes 3244032 | tf_op jit(solution)/shard_map/all_gather | solution.py:80
  273.1 3.1 copy-start.6
  273.2 2.9 collective-permute-start
  277.0 41.1 %collective-permute-start.1 = (bf16[128,384]{0,1:T(8,128)(2,1)S(1)}, bf16[128,384]{0,1:T(8,128)(2,1)S(1)}, u32[]{:S(2)}, u32[]{:S(2)}) collective-permute-start(bf16[128,384]{0,1:T(8,128)(2,1)S(1)} %get-tuple-element.53), channel_id=1, source_target_pairs={{256,0},{384,128},{257,1},{385,129},{258,2},{386,130},{259,3},{387... | collective-permute-start | bytes 294920 | tf_op jit(solution)/shard_map/ppermute | solution.py:12
Sparse Core Ops, SparseCore 0:
  10.6 118.3 all-gather.4
  131.0 131.0 all-gather.6
where the time goes:
time: 450 us
  waiting for transfers between devices  289 us (64%)
  blocking collectives  124 us (28%)
  between operations  14.2 us (3%)
  local copies, waits for them, and re-layouts  9.4 us (2%)
  matrix products  5.29 us (1%)
    all_gather x1, waiting for transfers between devices, local(): lax.all_gather(values, 'seq', axis=0, tiled=True)  133 us
    psum x1, blocking collectives, local(): total_gate = lax.psum(placed, ('segment', 'seq', 'dp'))  124 us
    all_gather x1, waiting for transfers between devices, local(): lax.all_gather(keys, 'seq', axis=0, tiled=True)  116 us
    ppermute x2, waiting for transfers between devices, shifted(): lax.ppermute(value, axis, [(source, source + steps) for source in range(f...  39.8 us
  transfers between devices with their start and end apart: 4, of which 4 were waited for; matrix products, arithmetic and copies ran while one was open for 1% of the time, Pallas kernels for 0%

commit v1 on v0

--- a/solution.py
+++ b/solution.py
@@ -77,7 +77,9 @@
     width_dev = queries.shape[1]
     all_keys, all_values = (
         lax.all_gather(keys, "seq", axis=0, tiled=True),
-        lax.all_gather(values, "seq", axis=0, tiled=True),
+        jnp.concatenate(
+            lax.all_to_all(jnp.stack([values] * lax.axis_size("seq")), "seq", 0, 0), axis=0
+        ),
     )
     gain_row = lax.dynamic_slice_in_dim(q_gain, section, 1, 0)[0]
     gate_part = lax.dynamic_slice_in_dim(gate, slot * width_dev, width_dev, 0)

time: 450 us -> 435 us (0.967)
  waiting for transfers between devices: 289 us -> 251 us
  starting transfers between devices: 2.67 us -> 19.8 us
  local copies, waits for them, and re-layouts: 9.4 us -> 22.6 us
  blocking collectives: 124 us -> 116 us
    all_to_all x0 -> x1, waiting for transfers between devices: none -> 149 us  [local(): lax.all_to_all(jnp.stack([values] * lax.axis_size('seq')), 'seq', 0, 0)]
    all_gather x1 -> x0, waiting for transfers between devices: 133 us -> none  [local(): lax.all_gather(values, 'seq', axis=0, tiled=True)]
    all_gather x1, waiting for transfers between devices: 116 us -> 54.8 us  [local(): lax.all_gather(keys, 'seq', axis=0, tiled=True)]
    all_to_all x0 -> x1, starting transfers between devices: none -> 17.2 us  [local(): lax.all_to_all(jnp.stack([values] * lax.axis_size('seq')), 'seq', 0, 0)]
    psum x1, blocking collectives: 124 us -> 116 us  [local(): total_gate = lax.psum(placed, ('segment', 'seq', 'dp'))]
    ppermute x2, waiting for transfers between devices: 39.8 us -> 47.1 us  [shifted(): lax.ppermute(value, axis, [(source, source + steps) for source in range(f...]
    another operation x2 -> x5, local copies, waits for them, and re-layouts: 0.67 us -> 7.01 us
where the time goes in v1:
time: 435 us; the launch traced here: 434 us
  waiting for transfers between devices  251 us (58%)
  blocking collectives  116 us (27%)
  local copies, waits for them, and re-layouts  22.6 us (5%)
  starting transfers between devices  19.8 us (5%)
  between operations  14.2 us (3%)
  matrix products  5.28 us (1%)
    all_to_all x1, waiting for transfers between devices, local(): lax.all_to_all(jnp.stack([values] * lax.axis_size('seq')), 'seq', 0, 0)  149 us
    psum x1, blocking collectives, local(): total_gate = lax.psum(placed, ('segment', 'seq', 'dp'))  116 us
    all_gather x1, waiting for transfers between devices, local(): lax.all_gather(keys, 'seq', axis=0, tiled=True)  54.8 us
    ppermute x2, waiting for transfers between devices, shifted(): lax.ppermute(value, axis, [(source, source + steps) for source in range(f...  47.1 us
    all_to_all x1, starting transfers between devices, local(): lax.all_to_all(jnp.stack([values] * lax.axis_size('seq')), 'seq', 0, 0)  17.2 us
  transfers between devices with their start and end apart: 4, of which 4 were waited for; matrix products, arithmetic and copies ran while one was open for 1% of the time, Pallas kernels for 0%

profile of v1, /device:TPU:1, one launch (start us, length us, event | category | flops | bytes accessed | tf_op | source)
XLA Modules:
  0.0 434.1 jit_solution(1822454851738424031)
XLA Ops:
  7.2 0.0 copy-start
  7.2 1.0 copy.23
  8.2 0.0 copy-start.14
  8.2 0.0 copy-start.15
  8.2 2.4 stack.3
  10.6 17.2 %all-to-all-start = ((bf16[32,128,384]{1,2,0:T(8,128)(2,1)}), bf16[32,128,384]{1,2,0:T(8,128)(2,1)}, u32[]{:S(2)}, u32[]{:S(2)}) async-start(bf16[32,128,384]{1,2,0:T(8,128)(2,1)} %stack.3), calls=%async_computation | async-start | bytes 6291456 | tf_op jit(solution)/shard_map/all_to_all | solution.py:81
  27.8 0.0 all-gather.3.cloned.1.call-start
  27.9 0.0 copy-done.14
  27.9 0.8 copy.22
  28.7 0.0 all-gather.3.cloned.1.call-update
  28.7 0.0 copy-done
  28.7 0.1 mul.127
  28.8 0.0 copy-done.15
  28.8 0.1 copy.21
  29.0 0.1 fusion.70
  29.2 0.1 dynamic_slice.11
  29.2 149.4 %all-to-all-done = bf16[32,128,384]{1,2,0:T(8,128)(2,1)} async-done(((bf16[32,128,384]{1,2,0:T(8,128)(2,1)}), bf16[32,128,384]{1,2,0:T(8,128)(2,1)}, u32[]{:S(2)}, u32[]{:S(2)}) %all-to-all-start) | async-done | bytes 3145760 | tf_op jit(solution)/shard_map/all_to_all | solution.py:81
  178.7 3.4 copy.24
  182.1 54.8 %all-gather.3.cloned.1.call-done = bf16[1,4096,384]{1,2,0:T(8,128)(2,1)} async-done(((bf16[1,128,384]{1,2,0:T(8,128)(2,1)}), bf16[1,4096,384]{1,2,0:T(8,128)(2,1)}) %all-gather.3.cloned.1.call-update) | async-done | bytes 3145744 | tf_op jit(solution)/shard_map/all_gather | solution.py:79
  236.9 21.3 %conditional.2 = (f32[128,384]{0,1:T(8,128)S(1)}, bf16[128,384]{1,0:T(8,128)(2,1)}) conditional(s32[]{:T(128)} %convert_element_type.105, (f32[128,384]{0,1:T(8,128)S(1)}, bf16[4096,384]{0,1:T(8,128)(2,1)}, bf16[4096,384]{1,0:T(8,128)(2,1)S(1)}) %tuple.76, () %tuple.30), branch_computations={%region_1.8_spmd, %region_8.9_spmd} | conditional | flops 824670720 | bytes 106642600 | solution.py:98
  236.9 3.5 fusion.71
  240.4 0.8 fusion.76
  241.3 1.9 copy-done.5
  243.2 0.7 fusion
  243.9 2.9 copy.25
  246.9 2.3 fusion.72
  249.2 0.8 copy-done.6
  250.0 0.9 fusion.39
  250.9 0.8 fusion.75
  251.8 0.7 fusion.2
  252.5 0.9 fusion.36
  253.4 0.8 fusion.74
  254.3 0.7 fusion.4
  255.0 0.9 fusion.33
  255.9 0.0 copy-start.13
  255.9 0.6 copy-done.13
  256.6 1.6 copy.30
  258.2 0.1 multiply_convert_fusion
  258.3 1.3 collective-permute-start
  259.6 1.6 collective-permute-done
  261.2 0.8 conditional.3
  261.2 0.6 broadcast.54.clone
  262.1 1.3 collective-permute-start.1
  263.4 1.6 select_bitcast_fusion
  265.0 45.5 %collective-permute-done.1 = bf16[128,384]{0,1:T(8,128)(2,1)S(1)} collective-permute-done((bf16[128,384]{0,1:T(8,128)(2,1)S(1)}, bf16[128,384]{0,1:T(8,128)(2,1)S(1)}, u32[]{:S(2)}, u32[]{:S(2)}) %collective-permute-start.1) | collective-permute-done | bytes 98336 | tf_op jit(solution)/shard_map/ppermute | solution.py:12
  310.4 0.1 multiply_reduce_fusion.3
  310.6 0.2 dynamic_update_slice.3
  310.9 116.4 %psum.7 = f32[768]{0:T(1024)} all-reduce(f32[768]{0:T(1024)S(1)} %dynamic_update_slice.3), channel_id=1, replica_groups=mesh['segment'=4,'seq'=32,'dp'=4] {'segment','seq','dp'}, use_global_device_ids=true, to_apply=%region_21.22 | all-reduce | flops 768 | bytes 6144 | tf_op jit(solution)/shard_map/psum | solution.py:122
  (19 shorter events, 0.1 us)
Async XLA Ops:
  7.2 21.5 %copy-start = (f32[2,64]{1,0:T(2,128)S(1)}, f32[2,64]{1,0:T(2,128)}, u32[]{:S(2)}) copy-start(f32[2,64]{1,0:T(2,128)} %param.13) | copy-start | bytes 1540
  8.2 19.7 %copy-start.14 = (bf16[1,128,384]{2,1,0:T(8,128)(2,1)S(1)}, bf16[1,128,384]{2,1,0:T(8,128)(2,1)}, u32[]{:S(2)}) copy-start(bf16[1,128,384]{2,1,0:T(8,128)(2,1)} %param.11) | copy-start | bytes 294916
  8.2 20.6 %copy-start.15 = (bf16[1,128,384]{2,1,0:T(8,128)(2,1)S(1)}, bf16[1,128,384]{2,1,0:T(8,128)(2,1)}, u32[]{:S(2)}) copy-start(bf16[1,128,384]{2,1,0:T(8,128)(2,1)} %param.10) | copy-start | bytes 294916
  10.6 18.5 %copy-start.22 = (f32[768]{0:T(1024)S(1)}, f32[768]{0:T(1024)}, u32[]{:S(2)}) copy-start(f32[768]{0:T(1024)} %param.14) | copy-start | bytes 9220
  10.6 168.0 %all-to-all-start = ((bf16[32,128,384]{1,2,0:T(8,128)(2,1)}), bf16[32,128,384]{1,2,0:T(8,128)(2,1)}, u32[]{:S(2)}, u32[]{:S(2)}) async-start(bf16[32,128,384]{1,2,0:T(8,128)(2,1)} %stack.3), calls=%async_computation | async-start | bytes 6291456 | tf_op jit(solution)/shard_map/all_to_all | solution.py:81
  27.8 209.0 %all-gather.3.cloned.1.call-start = ((), (), s32[]{:S(2)}) async-start(), calls=%async_computation.1 | async-start | bytes 3244032 | tf_op jit(solution)/shard_map/all_gather | solution.py:79
  241.3 1.9 copy-start.5
  246.8 3.1 copy-start.6
  249.2 1.7 copy-start.12
  251.8 1.7 copy-start.11
  255.9 0.6 copy-start.13
  258.3 2.9 collective-permute-start
  262.1 48.4 %collective-permute-start.1 = (bf16[128,384]{0,1:T(8,128)(2,1)S(1)}, bf16[128,384]{0,1:T(8,128)(2,1)S(1)}, u32[]{:S(2)}, u32[]{:S(2)}) collective-permute-start(bf16[128,384]{0,1:T(8,128)(2,1)S(1)} %get-tuple-element.53), channel_id=1, source_target_pairs={{256,0},{384,128},{257,1},{385,129},{258,2},{386,130},{259,3},{387... | collective-permute-start | bytes 294920 | tf_op jit(solution)/shard_map/ppermute | solution.py:12
Sparse Core Ops, SparseCore 0:
  31.3 205.5 all-gather.2
